TPU v7x, 32 devices: a whole 2x2x4 slice. The times are simulated.
32 devices in a mesh: row: 4 (over y, x), col: 8 (over z, core).
Axes of the slice: x: 2, y: 2, z: 4, core: 2. Of those that a mesh axis runs over, the one named last changes fastest.
Arguments:
- points: bfloat16 [8192, 256], P(('row', 'col')), may hold values from -0.4 to 0.4, as said below
- spread: float32 [8192], P(('row', 'col')), may hold values from 1 to 12
- vectors: bfloat16 [8192, 64], P(('row', 'col')), may hold values from -6 to 6
Outputs:
- product: float32 [8192, 64], P(('row', 'col'))
Inputs may be any that keep to these rules, and one draw needn't show every extreme that they name: `points`: embedding entries are real values of order 0.1.
All inputs are finite; a program needn't handle non-finite values.
Results may differ from a plain program's by a relative error of at most 0.0085.
Values may be sent and summed in bfloat16 or wider, within the bound.
A program may use at most 128 MiB of HBM per device.

v0:
```python
import jax
import jax.numpy as jnp
from jax import lax
from jax.sharding import PartitionSpec as P


def distances(left_pts, right_pts):
    left_f = left_pts.astype(jnp.float32)
    right_f = right_pts.astype(jnp.float32)
    left_sq = jnp.sum(left_f * left_f, axis=1)
    right_sq = jnp.sum(right_f * right_f, axis=1)
    cross = lax.dot_general(
        left_pts, right_pts, (((1,), (1,)), ((), ())), preferred_element_type=jnp.float32
    )
    return left_sq[:, None] + right_sq[None, :] - 2.0 * cross


def local(points, spread, vectors):
    share_rows = points.shape[0]
    n_rows = lax.axis_size("row")
    n_cols = lax.axis_size("col")
    row_pos = lax.axis_index("row")
    col_pos = lax.axis_index("col")
    blk_pts, blk_bw, blk_vec = (
        lax.all_gather(points, "col", axis=0, tiled=True),
        lax.all_gather(spread.astype(jnp.bfloat16), "col", axis=0, tiled=True).astype(spread.dtype),
        lax.all_gather(vectors, "col", axis=0, tiled=True),
    )
    crs_pts, crs_bw, crs_vec = (
        lax.all_gather(points, "row", axis=0, tiled=True),
        lax.all_gather(spread.astype(jnp.bfloat16), "row", axis=0, tiled=True).astype(spread.dtype),
        lax.all_gather(vectors, "row", axis=0, tiled=True),
    )
    blk_local = jnp.arange(share_rows * n_cols, dtype=jnp.int32)
    blk_ids = row_pos * (n_cols * share_rows) + blk_local
    crs_local = jnp.arange(share_rows * n_rows, dtype=jnp.int32)
    crs_ids = (
        crs_local // share_rows * (n_cols * share_rows)
        + col_pos * share_rows
        + crs_local % share_rows
    )
    same = blk_ids[:, None] == crs_ids[None, :]
    dist = distances(blk_pts, crs_pts)
    kernel = jnp.where(same, jnp.float32(0.0), jnp.exp(-blk_bw[:, None] * dist))
    totals = lax.psum(jnp.sum(kernel, axis=1), "col")
    norm = (kernel / totals[:, None]).astype(jnp.bfloat16)
    to_cross = lax.dot_general(
        norm, blk_vec, (((0,), (0,)), ((), ())), preferred_element_type=jnp.float32
    )
    mirror = jnp.where(same, jnp.float32(0.0), jnp.exp(-crs_bw[None, :] * dist))
    mirror_tot = lax.psum(jnp.sum(mirror, axis=0), "row")
    mirror_norm = (mirror / mirror_tot[None, :]).astype(jnp.bfloat16)
    to_cross = to_cross + lax.dot_general(
        mirror_norm, blk_vec, (((0,), (0,)), ((), ())), preferred_element_type=jnp.float32
    )
    summed = lax.psum_scatter(to_cross, "row", scatter_dimension=0, tiled=True)
    return 0.5 * summed


def solution(mesh):
    placed = (P(("row", "col"), None), P(("row", "col")), P(("row", "col"), None))
    return jax.shard_map(
        local, mesh=mesh, in_specs=placed, out_specs=P(("row", "col"), None), check_vma=False
    )
```

profile of v0, /device:TPU:0, one launch (start us, length us, event | category | flops | bytes accessed | tf_op | source)
XLA Modules:
  0.0 126.9 jit_solution(6512187139585747209)
XLA Ops:
  6.5 0.0 all-gather.4.cloned.1.call-start
  6.5 0.7 all-gather.4.cloned.1.call-update
  7.3 0.0 reduce-scatter.2.cloned.1.call-start
  7.3 0.7 convert_element_type.22
  8.0 9.5 %all-gather.1 = bf16[4,1,256]{2,1,0:T(2,128)(2,1)S(1)} all-gather(bf16[1,1,256]{2,1,0:T(2,128)(2,1)S(1)} %reshape.35), channel_id=1, replica_groups=mesh['row'=4,'col'=8] {'row'}, dimensions={0}, use_global_device_ids=true | all-gather | bytes 2560 | tf_op jit(solution)/shard_map/all_gather | solution.py:31
  17.5 12.0 %all-gather = bf16[8,1,256]{2,1,0:T(2,128)(2,1)S(1)} all-gather(bf16[1,1,256]{2,1,0:T(2,128)(2,1)S(1)} %reshape.35), channel_id=1, replica_groups=mesh['row'=4,'col'=8] {'col'}, dimensions={0}, use_global_device_ids=true | all-gather | bytes 4608 | tf_op jit(solution)/shard_map/all_gather | solution.py:26
  29.5 10.3 %all_gather.17 = bf16[1024,256]{1,0:T(8,128)(2,1)S(1)} all-gather(bf16[256,256]{1,0:T(8,128)(2,1)} %param.3), channel_id=1, replica_groups=mesh['row'=4,'col'=8] {'row'}, dimensions={0}, use_global_device_ids=true | all-gather | bytes 655360 | tf_op jit(solution)/shard_map/all_gather | solution.py:30
  39.8 14.4 %all_gather.18 = bf16[2048,64]{0,1:T(8,128)(2,1)S(1)} all-gather(bf16[256,64]{0,1:T(8,128)(2,1)} %param.5), channel_id=1, replica_groups=mesh['row'=4,'col'=8] {'col'}, dimensions={0}, use_global_device_ids=true | all-gather | bytes 294912 | tf_op jit(solution)/shard_map/all_gather | solution.py:27
  54.2 0.2 multiply_reduce_fusion.1
  54.5 0.0 all-gather.4.cloned.1.call-done
  54.5 1.6 %multiply_reduce_fusion = f32[2048]{0:T(1024)S(1)} fusion(bf16[2048,256]{1,0:T(8,128)(2,1)} %all-gather.4.cloned.1.call-done), kind=kLoop, calls=%fused_computation.9 | loop fusion | flops 1570816 | bytes 1056768 | tf_op jit(solution)/shard_map/reduce_sum | solution.py:10
  56.1 7.5 %fusion = (f32[2048]{0:T(1024)S(1)}, f32[1024]{0:T(1024)S(1)}, f32[2048,1024]{1,0:T(8,128)}) fusion(f32[1024]{0:T(1024)S(1)} %multiply_reduce_fusion.1, f32[2048]{0:T(1024)S(1)} %multiply_reduce_fusion, f32[2048]{0:T(1024)S(1)} %bitcast.6, s32[1024]{0:T(1024)S(1)} %fusion.13, s32[2048]{0:T(1024)S(1)} %iota_add_fusion, f32[1024]{0:T(1024)S(1)} %bitcast.8, ...), kind=kOutput, calls=%fused_computation.5 | convolution fusion | flops 1094710272 | bytes 10010624 | tf_op jit(solution)/shard_map/dot_general | solution.py:12
  63.6 8.9 %psum.15 = f32[1024]{0:T(1024)S(1)} all-reduce(f32[1024]{0:T(1024)S(1)} %get-tuple-element.6), channel_id=1, replica_groups=mesh['row'=4,'col'=8] {'row'}, use_global_device_ids=true, to_apply=%region_5.6 | all-reduce | flops 1024 | bytes 8192 | tf_op jit(solution)/shard_map/psum | solution.py:51
  72.5 13.9 %psum.14 = f32[2048]{0:T(1024)S(1)} all-reduce(f32[2048]{0:T(1024)S(1)} %get-tuple-element.5), channel_id=1, replica_groups=mesh['row'=4,'col'=8] {'col'}, use_global_device_ids=true, to_apply=%region_3.4 | all-reduce | flops 2048 | bytes 16384 | tf_op jit(solution)/shard_map/psum | solution.py:45
  86.4 0.0 copy-start
  86.4 6.9 %fusion.2 = f32[1024,64]{0,1:T(8,128)S(1)} fusion(bf16[2048,64]{0,1:T(8,128)(2,1)S(1)} %all_gather.18, f32[2048,1024]{1,0:T(8,128)} %get-tuple-element.7, f32[1024]{0:T(1024)S(1)} %psum.15, f32[1024]{0:T(1024)S(1)} %bitcast.9, f32[1024]{0:T(1024)S(1)} %multiply_reduce_fusion.1, f32[2048]{0:T(1024)S(1)} %multiply_reduce_fusion, s32[1024]{0:T(1024)S(1)} %fusion.13, ...), kind=kOutput, calls=%fused_computation.7 | convolution fusion | flops 285212672 | bytes 8945664 | tf_op jit(solution)/shard_map/dot_general | solution.py:53
  93.3 0.0 copy-done
  93.3 3.8 %fusion.4 = f32[1024,64]{0,1:T(8,128)} fusion(f32[1024,64]{0,1:T(8,128)S(1)} %fusion.2, bf16[2048,64]{0,1:T(8,128)(2,1)S(1)} %all_gather.18, f32[2048,1024]{1,0:T(8,128)S(1)} %copy-done, f32[2048]{0:T(1024)S(1)} %psum.14, f32[1024]{0:T(1024)S(1)} %multiply_reduce_fusion.1, f32[2048]{0:T(1024)S(1)} %multiply_reduce_fusion, f32[2048]{0:T(1024)S(1)} %bitcast.7, ...), kind=kOutput, calls=%fused_computation.10 | convolution fusion | flops 285278208 | bytes 9216000 | tf_op jit(solution)/shard_map/dot_general | solution.py:47
  97.1 0.0 reduce-scatter.2.cloned.1.call-update
  97.2 21.5 %reduce-scatter.2.cloned.1.call-done = f32[256,64]{0,1:T(8,128)} async-done(((f32[1024,64]{0,1:T(8,128)}), f32[256,64]{0,1:T(8,128)}) %reduce-scatter.2.cloned.1.call-update) | async-done | bytes 65552 | tf_op jit(solution)/shard_map/reduce_scatter | solution.py:56
  118.6 1.5 %broadcast_multiply_fusion = f32[256,64]{0,1:T(8,128)} fusion(f32[256,64]{0,1:T(8,128)} %reduce-scatter.2.cloned.1.call-done), kind=kLoop, calls=%fused_computation.12 | loop fusion | flops 16384 | bytes 131072 | tf_op jit(solution)/shard_map/mul | solution.py:57
  (5 shorter events, 0.0 us)
Async XLA Ops:
  6.5 47.9 %all-gather.4.cloned.1.call-start = ((), (), s32[]{:S(2)}) async-start(), calls=%async_computation.1 | async-start | bytes 1179648 | tf_op jit(solution)/shard_map/all_gather | solution.py:25
  7.3 111.4 %reduce-scatter.2.cloned.1.call-start = ((), (), s32[]{:S(2)}) async-start(), calls=%async_computation.2 | async-start | bytes 327680 | tf_op jit(solution)/shard_map/reduce_scatter | solution.py:56
  86.4 6.9 %copy-start = (f32[2048,1024]{1,0:T(8,128)S(1)}, f32[2048,1024]{1,0:T(8,128)}, u32[]{:S(2)}) copy-start(f32[2048,1024]{1,0:T(8,128)} %get-tuple-element.7) | copy-start | bytes 25165828
Sparse Core Ops, SparseCore 0:
  9.0 24.7 all-gather.3
  97.3 21.3 reduce-scatter.1
where the time goes:
time: 127 us
  blocking collectives  69 us (54%)
  waiting for transfers between devices  22.2 us (17%)
  matrix products  18.2 us (14%)
  between operations  13.5 us (11%)
  other arithmetic  3.97 us (3%)
    reduce_scatter x1, waiting for transfers between devices, local(): summed = lax.psum_scatter(to_cross, 'row', scatter_dimension=0, tiled=True)  21.5 us
    all_gather x1, blocking collectives, local(): lax.all_gather(vectors, 'col', axis=0, tiled=True)  14.4 us
    psum x1, blocking collectives, local(): totals = lax.psum(jnp.sum(kernel, axis=1), 'col')  13.9 us
    all_gather x1, blocking collectives, local(): lax.all_gather(spread.astype(jnp.bfloat16), 'col', axis=0, tiled=True)  12 us
    all_gather x1, blocking collectives, local(): lax.all_gather(points, 'row', axis=0, tiled=True)  10.3 us
    all_gather x1, blocking collectives, local(): lax.all_gather(spread.astype(jnp.bfloat16), 'row', axis=0, tiled=True)  9.5 us
    psum x1, blocking collectives, local(): mirror_tot = lax.psum(jnp.sum(mirror, axis=0), 'row')  8.9 us
    dot_general x1, matrix products, distances(): lax.dot_general(left_pts, right_pts, (((1,), (1,)), ((), ())), preferred_...  7.5 us
  transfers between devices with their start and end apart: 2, of which 1 were waited for; matrix products, arithmetic and copies ran while one was open for 1% of the time, Pallas kernels for 0%

commit v1 on v0

--- a/solution.py
+++ b/solution.py
@@ -42,7 +42,9 @@
     same = blk_ids[:, None] == crs_ids[None, :]
     dist = distances(blk_pts, crs_pts)
     kernel = jnp.where(same, jnp.float32(0.0), jnp.exp(-blk_bw[:, None] * dist))
-    totals = lax.psum(jnp.sum(kernel, axis=1), "col")
+    a0 = jnp.sum(kernel, axis=1)
+    v1 = lax.all_gather(a0, "col")
+    totals = jnp.sum(v1, axis=0)
     norm = (kernel / totals[:, None]).astype(jnp.bfloat16)
     to_cross = lax.dot_general(
         norm, blk_vec, (((0,), (0,)), ((), ())), preferred_element_type=jnp.float32

time: 127 us -> 127 us (level)
    all_gather x0 -> x1, blocking collectives: none -> 14 us  [local(): v1 = lax.all_gather(a0, 'col')]
    psum x1 -> x0, blocking collectives: 13.9 us -> none  [local(): totals = lax.psum(jnp.sum(kernel, axis=1), 'col')]
where the time goes in v1:
time: 127 us
  blocking collectives  69.1 us (54%)
  waiting for transfers between devices  22.2 us (17%)
  matrix products  18.2 us (14%)
  between operations  13.5 us (11%)
  other arithmetic  3.99 us (3%)
    reduce_scatter x1, waiting for transfers between devices, local(): summed = lax.psum_scatter(to_cross, 'row', scatter_dimension=0, tiled=True)  21.5 us
    all_gather x1, blocking collectives, local(): lax.all_gather(vectors, 'col', axis=0, tiled=True)  14.4 us
    all_gather x1, blocking collectives, local(): v1 = lax.all_gather(a0, 'col')  14 us
    all_gather x1, blocking collectives, local(): lax.all_gather(spread.astype(jnp.bfloat16), 'col', axis=0, tiled=True)  12 us
    all_gather x1, blocking collectives, local(): lax.all_gather(points, 'row', axis=0, tiled=True)  10.3 us
    all_gather x1, blocking collectives, local(): lax.all_gather(spread.astype(jnp.bfloat16), 'row', axis=0, tiled=True)  9.5 us
    psum x1, blocking collectives, local(): mirror_tot = lax.psum(jnp.sum(mirror, axis=0), 'row')  8.91 us
    dot_general x1, matrix products, distances(): lax.dot_general(left_pts, right_pts, (((1,), (1,)), ((), ())), preferred_...  7.49 us
  transfers between devices with their start and end apart: 2, of which 1 were waited for; matrix products, arithmetic and copies ran while one was open for 1% of the time, Pallas kernels for 0%

profile of v1, /device:TPU:0, one launch (start us, length us, event | category | flops | bytes accessed | tf_op | source)
XLA Modules:
  0.0 127.0 jit_solution(3339929738409985810)
XLA Ops:
  6.5 0.0 all-gather.5.cloned.1.call-start
  6.5 0.7 all-gather.5.cloned.1.call-update
  7.3 0.0 reduce-scatter.2.cloned.1.call-start
  7.3 0.7 convert_element_type.22
  8.0 9.5 %all-gather.2 = bf16[4,1,256]{2,1,0:T(2,128)(2,1)S(1)} all-gather(bf16[1,1,256]{2,1,0:T(2,128)(2,1)S(1)} %reshape.36), channel_id=1, replica_groups=mesh['row'=4,'col'=8] {'row'}, dimensions={0}, use_global_device_ids=true | all-gather | bytes 2560 | tf_op jit(solution)/shard_map/all_gather | solution.py:31
  17.5 12.0 %all-gather.1 = bf16[8,1,256]{2,1,0:T(2,128)(2,1)S(1)} all-gather(bf16[1,1,256]{2,1,0:T(2,128)(2,1)S(1)} %reshape.36), channel_id=1, replica_groups=mesh['row'=4,'col'=8] {'col'}, dimensions={0}, use_global_device_ids=true | all-gather | bytes 4608 | tf_op jit(solution)/shard_map/all_gather | solution.py:26
  29.5 10.3 %all_gather.23 = bf16[1024,256]{1,0:T(8,128)(2,1)S(1)} all-gather(bf16[256,256]{1,0:T(8,128)(2,1)} %param.3), channel_id=1, replica_groups=mesh['row'=4,'col'=8] {'row'}, dimensions={0}, use_global_device_ids=true | all-gather | bytes 655360 | tf_op jit(solution)/shard_map/all_gather | solution.py:30
  39.8 14.4 %all_gather.26 = bf16[2048,64]{0,1:T(8,128)(2,1)S(1)} all-gather(bf16[256,64]{0,1:T(8,128)(2,1)} %param.5), channel_id=1, replica_groups=mesh['row'=4,'col'=8] {'col'}, dimensions={0}, use_global_device_ids=true | all-gather | bytes 294912 | tf_op jit(solution)/shard_map/all_gather | solution.py:27
  54.2 0.2 multiply_reduce_fusion.1
  54.5 0.0 all-gather.5.cloned.1.call-done
  54.5 1.6 %multiply_reduce_fusion = f32[2048]{0:T(1024)S(1)} fusion(bf16[2048,256]{1,0:T(8,128)(2,1)} %all-gather.5.cloned.1.call-done), kind=kLoop, calls=%fused_computation.9 | loop fusion | flops 1570816 | bytes 1056768 | tf_op jit(solution)/shard_map/reduce_sum | solution.py:10
  56.1 7.5 %fusion = (f32[2048]{0:T(1024)S(1)}, f32[1024]{0:T(1024)S(1)}, f32[2048,1024]{1,0:T(8,128)}) fusion(f32[1024]{0:T(1024)S(1)} %multiply_reduce_fusion.1, f32[2048]{0:T(1024)S(1)} %multiply_reduce_fusion, f32[2048]{0:T(1024)S(1)} %bitcast.6, s32[1024]{0:T(1024)S(1)} %fusion.13, s32[2048]{0:T(1024)S(1)} %iota_add_fusion, f32[1024]{0:T(1024)S(1)} %bitcast.8, ...), kind=kOutput, calls=%fused_computation.5 | convolution fusion | flops 1094710272 | bytes 10010624 | tf_op jit(solution)/shard_map/dot_general | solution.py:12
  63.6 8.9 %psum.7 = f32[1024]{0:T(1024)S(1)} all-reduce(f32[1024]{0:T(1024)S(1)} %get-tuple-element.6), channel_id=1, replica_groups=mesh['row'=4,'col'=8] {'row'}, use_global_device_ids=true, to_apply=%region_5.6 | all-reduce | flops 1024 | bytes 8192 | tf_op jit(solution)/shard_map/psum | solution.py:53
  72.5 14.0 %all-gather = f32[16384]{0:T(1024)S(1)} all-gather(f32[2048]{0:T(1024)S(1)} %get-tuple-element.5), channel_id=2, replica_groups=mesh['row'=4,'col'=8] {'col'}, dimensions={0}, use_global_device_ids=true | all-gather | bytes 73728 | tf_op jit(solution)/shard_map/all_gather | solution.py:46
  86.5 0.0 copy-start
  86.5 6.9 %fusion.2 = f32[1024,64]{0,1:T(8,128)S(1)} fusion(bf16[2048,64]{0,1:T(8,128)(2,1)S(1)} %all_gather.26, f32[2048,1024]{1,0:T(8,128)} %get-tuple-element.7, f32[1024]{0:T(1024)S(1)} %psum.7, f32[1024]{0:T(1024)S(1)} %bitcast.9, f32[1024]{0:T(1024)S(1)} %multiply_reduce_fusion.1, f32[2048]{0:T(1024)S(1)} %multiply_reduce_fusion, s32[1024]{0:T(1024)S(1)} %fusion.13, ...), kind=kOutput, calls=%fused_computation.7 | convolution fusion | flops 285212672 | bytes 8945664 | tf_op jit(solution)/shard_map/dot_general | solution.py:55
  93.4 0.0 copy-done
  93.4 3.8 %fusion.4 = f32[1024,64]{0,1:T(8,128)} fusion(f32[1024,64]{0,1:T(8,128)S(1)} %fusion.2, bf16[2048,64]{0,1:T(8,128)(2,1)S(1)} %all_gather.26, f32[2048,1024]{1,0:T(8,128)S(1)} %copy-done, f32[2048]{0:T(1024)S(1)} %reduce_sum.48, f32[1024]{0:T(1024)S(1)} %multiply_reduce_fusion.1, f32[2048]{0:T(1024)S(1)} %multiply_reduce_fusion, f32[2048]{0:T(1024)S(1)} %bitcast.7, ...), kind=kOutput, calls=%fused_computation.10 | convolution fusion | flops 285278208 | bytes 9216000 | tf_op jit(solution)/shard_map/dot_general | solution.py:49
  97.2 0.0 reduce-scatter.2.cloned.1.call-update
  97.3 21.5 %reduce-scatter.2.cloned.1.call-done = f32[256,64]{0,1:T(8,128)} async-done(((f32[1024,64]{0,1:T(8,128)}), f32[256,64]{0,1:T(8,128)}) %reduce-scatter.2.cloned.1.call-update) | async-done | bytes 65552 | tf_op jit(solution)/shard_map/reduce_scatter | solution.py:58
  118.7 1.5 %broadcast_multiply_fusion = f32[256,64]{0,1:T(8,128)} fusion(f32[256,64]{0,1:T(8,128)} %reduce-scatter.2.cloned.1.call-done), kind=kLoop, calls=%fused_computation.12 | loop fusion | flops 16384 | bytes 131072 | tf_op jit(solution)/shard_map/mul | solution.py:59
  (7 shorter events, 0.1 us)
Async XLA Ops:
  6.5 47.9 %all-gather.5.cloned.1.call-start = ((), (), s32[]{:S(2)}) async-start(), calls=%async_computation.1 | async-start | bytes 1179648 | tf_op jit(solution)/shard_map/all_gather | solution.py:25
  7.3 111.5 %reduce-scatter.2.cloned.1.call-start = ((), (), s32[]{:S(2)}) async-start(), calls=%async_computation.2 | async-start | bytes 327680 | tf_op jit(solution)/shard_map/reduce_scatter | solution.py:58
  86.5 6.9 %copy-start = (f32[2048,1024]{1,0:T(8,128)S(1)}, f32[2048,1024]{1,0:T(8,128)}, u32[]{:S(2)}) copy-start(f32[2048,1024]{1,0:T(8,128)} %get-tuple-element.7) | copy-start | bytes 25165828
Sparse Core Ops, SparseCore 0:
  9.0 24.7 all-gather.4
  97.4 21.3 reduce-scatter.1
